TPU v7x, 512 devices: a whole 4x8x8 slice. The times are simulated.
512 devices in a mesh: wide: 64 (over y, z_lo, core), narrow: 8 (over x, z_hi).
Axes of the slice: x: 4, y: 8, z: 8 (z_hi: 2, z_lo: 4; z = z_hi * 4 + z_lo), core: 2. Of those that a mesh axis runs over, the one named last changes fastest.
Arguments:
- loads: float32 [2048, 24, 128], P(('wide', 'narrow')), may hold values from -6 to 6
- diagonal: float32 [2048, 128], P(('wide', 'narrow')), may hold values from 2 to 7
- stiffness: float32 [2048, 4, 128, 128], P(('wide', 'narrow')), may hold values from 0 to 0.001953125
- neighbors: int32 [2048, 4], P(('wide', 'narrow')), may hold values from 0 to 7
- slot_mask: int32 [2048, 4], P(('wide', 'narrow')), may hold values 0 or 1
- send_list: int32 [2048], P(('wide', 'narrow')), may hold values from 0 to 3
- aggregate: int32 [2048, 128], P(('wide', 'narrow')), may hold values from 0 to 127
- coarse_inverse: float32 [8192, 8192], P(('wide', 'narrow')), may hold values from -0.0078125 to 0.0078125
Outputs:
- correction: float32 [2048, 24, 128], P(('wide', 'narrow'))
- residual: float32 [2048, 24, 128], P(('wide', 'narrow'))
Inputs may be any that keep to these rules, and one draw needn't show every extreme that they name: `neighbors`: indices into the extended list of the block's group. `send_list`: block indices within the sending group. aggregate indices among the 128 aggregates of the particle's wide coordinate.
All inputs are finite; a program needn't handle non-finite values. No bound on the sum of `slot_mask` on one device may be relied on, other than what follows from the above.
Results may differ from a plain program's by a relative error of at most 0.00025.
Values sent between devices are 32-bit elements; how exact they have to be, the bound alone decides.
A program may use at most 64 MiB of HBM per device.

v0:
```python
import jax
import jax.numpy as jnp
from jax import lax
from jax.sharding import PartitionSpec as P

SWEEPS = 2
highest = lax.Precision.HIGHEST


def with_halo(block, sides, width):
    for axis, dim in sides:
        count = lax.axis_size(axis)
        forward = [(i, i + 1) for i in range(count - 1)]
        backward = [(target, source) for source, target in forward]
        low = lax.ppermute(
            lax.slice_in_dim(block, block.shape[dim] - width, None, axis=dim), axis, forward
        )
        high = lax.ppermute(lax.slice_in_dim(block, 0, width, axis=dim), axis, backward)
        block = jnp.concatenate([low, block, high], axis=dim)
    return block


def shards(loads, diagonal, stiffness, neighbors, slot_mask, send_list, aggregate, coarse_inverse):
    ghost_rows = send_list.shape[0] // 2
    live_slots = slot_mask.astype(jnp.float32)
    diag_rows = diagonal[:, None, :]

    def operate(vector):
        outgoing = jnp.take(vector, send_list, axis=0)
        padded = with_halo(outgoing, (("wide", 0),), ghost_rows)
        extended = jnp.concatenate([vector, padded[:ghost_rows], padded[3 * ghost_rows :]], axis=0)
        gathered = jnp.take(extended, neighbors, axis=0) * live_slots[:, :, None, None]
        coupled = jnp.einsum("bscj,bsij->bci", gathered, stiffness, precision=highest)
        return diag_rows * vector - coupled

    scaled = loads / diag_rows
    row_sums = jnp.sum(jnp.sum(jnp.abs(stiffness), axis=3) * live_slots[:, :, None], axis=1)
    local_peak = jnp.max(row_sums / diagonal)
    upper_bound = 1.0 + lax.pmax(local_peak, ("wide", "narrow"))
    centre = 0.625 * upper_bound
    direction = scaled / centre
    applied = operate(direction)
    half_span = 0.375 * upper_bound
    spread_ratio = 5.0 / 3.0
    weight_prev = 0.6
    solution = direction
    remainder = loads
    for sweep_index in range(SWEEPS):
        if sweep_index > 0:
            applied = operate(direction)
        remainder = remainder - applied
        weight_now = 1.0 / (2.0 * spread_ratio - weight_prev)
        direction = (
            weight_now * weight_prev * direction
            + 2.0 * weight_now / half_span * remainder / diag_rows
        )
        solution = solution + direction
        weight_prev = weight_now
    residual = remainder - operate(direction)
    agg_cols = coarse_inverse.shape[0] * lax.axis_size("narrow")
    one_hot = (
        aggregate[:, :, None] == jnp.arange(agg_cols, dtype=jnp.int32)[None, None, :]
    ).astype(jnp.float32)
    part_sums = jnp.einsum("bci,big->cg", residual, one_hot, precision=highest)
    owned_sums = lax.psum_scatter(part_sums, "narrow", scatter_dimension=1, tiled=True)
    coarse_own = jnp.einsum(
        "ch,kh->ck",
        lax.all_gather(owned_sums, ("wide", "narrow"), axis=1, tiled=True),
        coarse_inverse,
        precision=highest,
    )
    coarse_group = lax.all_gather(coarse_own, "narrow", axis=1, tiled=True)
    spread_back = jnp.einsum("cg,big->bci", coarse_group, one_hot, precision=highest)
    return (solution + spread_back, residual)


def solution(mesh):
    return jax.shard_map(
        shards,
        mesh=mesh,
        in_specs=(
            P(("wide", "narrow"), None, None),
            P(("wide", "narrow"), None),
            P(("wide", "narrow"), None, None, None),
            P(("wide", "narrow"), None),
            P(("wide", "narrow"), None),
            P(("wide", "narrow")),
            P(("wide", "narrow"), None),
            P(("wide", "narrow"), None),
        ),
        out_specs=(P(("wide", "narrow"), None, None), P(("wide", "narrow"), None, None)),
        check_vma=False,
    )
```

profile of v0, /device:TPU:8, one launch (start us, length us, event | category | flops | bytes accessed | tf_op | source)
XLA Modules:
  0.0 1646.6 jit_solution(16821099746210735129)
XLA Ops:
  7.2 0.0 copy-start
  7.2 0.0 copy-start.1
  7.2 0.0 copy-start.3
  7.2 0.0 copy-start.5
  7.2 0.0 reduce-scatter.4.cloned.1.call-start
  7.3 0.8 compare_and_fusion.1
  8.0 0.7 compare_select_fusion.1
  8.7 0.7 convert_element_type.4
  9.4 1.6 abs_reduce_fusion
  10.9 0.1 multiply_reduce_fusion
  11.0 1.3 divide_reduce_fusion
  12.3 104.9 %pmax.7 = f32[]{:T(128)} all-reduce(f32[]{:T(128)} %divide_reduce_fusion), channel_id=1, replica_groups=mesh['wide'=64,'narrow'=8] {'wide','narrow'}, use_global_device_ids=true, to_apply=%region_3.0 | all-reduce | flops 1 | bytes 8 | tf_op jit(solution)/shard_map/pmax | solution.py:39
  117.9 0.7 broadcast_multiply_fusion
  118.5 0.8 broadcast_divide_fusion
  119.4 0.6 gather_fusion
  119.9 0.1 broadcast_select_fusion.2
  120.0 1.9 collective-permute-start
  121.9 6.3 collective-permute-start.1
  128.3 0.7 compare_and_fusion
  129.0 0.7 compare_select_fusion
  129.6 0.1 reshape.77
  129.8 0.0 collective-permute-done
  129.8 0.0 collective-permute-done.1
  129.8 0.6 gather_fusion.1
  130.4 2.3 divide_add_fusion.1
  132.7 0.6 gather_fusion.2
  133.2 0.1 broadcast_select_fusion.1
  133.3 1.9 collective-permute-start.2
  135.2 6.3 collective-permute-start.3
  141.6 0.0 collective-permute-done.2
  141.6 1.4 collective-permute-done.3
  143.1 0.6 gather_fusion.3
  143.7 0.0 copy-done.1
  143.7 0.0 copy-done.3
  143.7 1.0 divide_add_fusion
  144.7 0.6 gather_fusion.4
  145.3 0.1 broadcast_select_fusion
  145.4 1.9 collective-permute-start.4
  147.3 6.3 collective-permute-start.5
  153.6 0.0 collective-permute-done.4
  153.7 1.5 collective-permute-done.5
  155.1 0.6 gather_fusion.5
  155.7 1.0 fusion.6
  156.7 0.0 copy-done.5
  156.7 0.0 copy-start.4
  156.8 1.1 convolution_bitcast_fusion
  157.9 0.0 reduce-scatter.4.cloned.1.call-update
  157.9 87.4 %reduce-scatter.4.cloned.1.call-done = f32[16,24]{1,0:T(8,128)} async-done(((f32[128,24]{1,0:T(8,128)}), f32[16,24]{1,0:T(8,128)}) %reduce-scatter.4.cloned.1.call-update) | async-done | bytes 1552
  245.3 0.0 copy-start.2
  245.3 1344.6 %all_gather.6 = f32[24,8192]{0,1:T(8,128)S(1)} all-gather(f32[24,16]{0,1:T(8,128)} %bitcast.46), channel_id=1, replica_groups=mesh['wide'=64,'narrow'=8] {'wide','narrow'}, dimensions={1}, use_global_device_ids=true | all-gather | bytes 787968 | tf_op jit(solution)/shard_map/all_gather | solution.py:68
  1590.0 0.0 copy-done
  1590.0 2.4 fusion.25
  1592.4 0.0 copy-done.4
  1592.4 46.4 %all_gather.7 = f32[24,128]{0,1:T(8,128)S(1)} all-gather(f32[24,16]{0,1:T(8,128)S(1)} %fusion.25), channel_id=1, replica_groups=mesh['wide'=64,'narrow'=8] {'narrow'}, dimensions={1}, use_global_device_ids=true | all-gather | bytes 13824 | tf_op jit(solution)/shard_map/all_gather | solution.py:72
  1638.7 0.0 copy-done.2
  1638.7 1.0 fusion
  (8 shorter events, 0.1 us)
Async XLA Ops:
  7.2 1582.8 %copy-start = (f32[16,8192]{1,0:T(8,128)S(1)}, f32[16,8192]{1,0:T(8,128)}, u32[]{:S(2)}) copy-start(f32[16,8192]{1,0:T(8,128)} %param.19) | copy-start | bytes 1572868
  7.2 136.5 %copy-start.1 = (f32[4,4,128,128]{3,2,1,0:T(8,128)S(1)}, f32[4,4,128,128]{3,2,1,0:T(8,128)}, u32[]{:S(2)}) copy-start(f32[4,4,128,128]{3,2,1,0:T(8,128)} %param.14) | copy-start | bytes 3145732
  7.2 136.5 %copy-start.3 = (f32[4,128]{1,0:T(4,128)S(1)}, f32[4,128]{1,0:T(4,128)}, u32[]{:S(2)}) copy-start(f32[4,128]{1,0:T(4,128)} %param.13) | copy-start | bytes 6148
  7.2 149.5 %copy-start.5 = (s32[4,128]{1,0:T(4,128)S(1)}, s32[4,128]{1,0:T(4,128)}, u32[]{:S(2)}) copy-start(s32[4,128]{1,0:T(4,128)} %param.18) | copy-start | bytes 6148
  7.2 238.1 %reduce-scatter.4.cloned.1.call-start = ((), (), s32[]{:S(2)}) async-start(), calls=%async_computation.1 | async-start | bytes 73728
  120.0 9.8 collective-permute-start
  121.9 7.9 collective-permute-start.1
  133.3 8.3 collective-permute-start.2
  135.2 7.8 collective-permute-start.3
  145.4 8.3 collective-permute-start.4
  147.3 7.8 collective-permute-start.5
  156.7 1435.6 %copy-start.4 = (f32[4,24,128]{2,1,0:T(8,128)}, f32[4,24,128]{2,1,0:T(8,128)S(1)}, u32[]{:S(2)}) copy-start(f32[4,24,128]{2,1,0:T(8,128)S(1)} %fusion.6) | copy-start | bytes 147460
  245.3 1393.4 %copy-start.2 = (f32[4,24,128]{2,1,0:T(8,128)S(1)}, f32[4,24,128]{2,1,0:T(8,128)}, u32[]{:S(2)}) copy-start(f32[4,24,128]{2,1,0:T(8,128)} %param.12) | copy-start | bytes 147460
Sparse Core Ops, SparseCore 0:
  158.0 87.2 reduce-scatter.3
where the time goes:
time: 1650 us
  blocking collectives  1500 us (91%)
  waiting for transfers between devices  90.4 us (5%)
  starting transfers between devices  24.8 us (2%)
    all_gather x1, blocking collectives, shards(): lax.all_gather(owned_sums, ('wide', 'narrow'), axis=1, tiled=True)  1340 us
    pmax x1, blocking collectives, shards(): upper_bound = 1.0 + lax.pmax(local_peak, ('wide', 'narrow'))  105 us
    unnamed x2, waiting for transfers between devices  87.4 us
    all_gather x1, blocking collectives, shards(): coarse_group = lax.all_gather(coarse_own, 'narrow', axis=1, tiled=True)  46.4 us
  transfers between devices with their start and end apart: 7, of which 3 were waited for; matrix products, arithmetic and copies ran while one was open for 0% of the time, Pallas kernels for 0%

commit v1 on v0

--- a/solution.py
+++ b/solution.py
@@ -5,6 +5,13 @@
 
 SWEEPS = 2
 highest = lax.Precision.HIGHEST
+
+
+def gather_over(x, axis, along):
+    size = lax.axis_size(axis)
+    blocks = jnp.stack([x for _ in range(size)])
+    blocks = lax.all_to_all(blocks, axis, split_axis=0, concat_axis=0)
+    return jnp.concatenate(blocks, axis=along)
 
 
 def with_halo(block, sides, width):
@@ -69,7 +76,7 @@
         coarse_inverse,
         precision=highest,
     )
-    coarse_group = lax.all_gather(coarse_own, "narrow", axis=1, tiled=True)
+    coarse_group = gather_over(coarse_own, "narrow", 1)
     spread_back = jnp.einsum("cg,big->bci", coarse_group, one_hot, precision=highest)
     return (solution + spread_back, residual)
 

time: 1650 us -> 1620 us (0.982)
  the two profiles are of different devices: /device:TPU:8 before, /device:TPU:32 now
where the time goes in v1:
time: 1620 us
  blocking collectives  1470 us (91%)
  waiting for transfers between devices  88 us (5%)
  starting transfers between devices  28.4 us (2%)
    all_gather x1, blocking collectives, shards(): lax.all_gather(owned_sums, ('wide', 'narrow'), axis=1, tiled=True)  1350 us
    pmax x1, blocking collectives, shards(): upper_bound = 1.0 + lax.pmax(local_peak, ('wide', 'narrow'))  103 us
    unnamed x2, waiting for transfers between devices  85.1 us
  transfers between devices with their start and end apart: 7, of which 3 were waited for; matrix products, arithmetic and copies ran while one was open for 0% of the time, Pallas kernels for 0%

profile of v1, /device:TPU:32, one launch (start us, length us, event | category | flops | bytes accessed | tf_op | source)
XLA Modules:
  0.0 1622.2 jit_solution(11339732329270046076)
XLA Ops:
  7.2 0.0 copy-start
  7.2 0.0 copy-start.1
  7.2 0.0 copy-start.3
  7.2 0.0 copy-start.5
  7.2 0.0 reduce-scatter.4.cloned.1.call-start
  7.3 0.8 convert_element_type.4
  8.0 1.6 abs_reduce_fusion
  9.6 0.7 compare_select_fusion.1
  10.3 0.1 multiply_reduce_fusion
  10.4 1.3 divide_reduce_fusion
  11.7 0.7 compare_and_fusion.1
  12.3 103.4 %pmax.7 = f32[]{:T(128)} all-reduce(f32[]{:T(128)} %divide_reduce_fusion), channel_id=1, replica_groups=mesh['wide'=64,'narrow'=8] {'wide','narrow'}, use_global_device_ids=true, to_apply=%region_3.0 | all-reduce | flops 1 | bytes 8 | tf_op jit(solution)/shard_map/pmax | solution.py:46
  116.3 0.7 broadcast_multiply_fusion
  117.0 0.8 broadcast_divide_fusion
  117.8 0.6 gather_fusion
  118.4 0.1 broadcast_select_fusion.2
  118.5 1.9 collective-permute-start
  120.4 7.5 collective-permute-start.1
  128.0 0.7 compare_select_fusion
  128.7 0.7 compare_and_fusion
  129.3 0.1 reshape.87
  129.5 0.0 collective-permute-done
  129.5 0.0 collective-permute-done.1
  129.5 0.6 gather_fusion.1
  130.1 2.3 divide_add_fusion.1
  132.4 0.6 gather_fusion.2
  132.9 0.1 broadcast_select_fusion.1
  133.0 1.9 collective-permute-start.2
  134.9 7.5 collective-permute-start.3
  142.5 0.0 collective-permute-done.2
  142.6 1.4 collective-permute-done.3
  144.0 0.6 gather_fusion.3
  144.6 0.0 copy-done.1
  144.6 0.0 copy-done.3
  144.6 1.0 divide_add_fusion
  145.6 0.6 gather_fusion.4
  146.2 0.1 broadcast_select_fusion
  146.3 1.9 collective-permute-start.4
  148.2 7.6 collective-permute-start.5
  155.8 0.0 collective-permute-done.4
  155.8 1.5 collective-permute-done.5
  157.3 0.6 gather_fusion.5
  157.8 1.0 fusion.6
  158.8 0.0 copy-done.5
  158.9 0.0 copy-start.4
  158.9 1.1 convolution_bitcast_fusion
  160.0 0.0 reduce-scatter.4.cloned.1.call-update
  160.0 85.0 %reduce-scatter.4.cloned.1.call-done = f32[16,24]{1,0:T(8,128)} async-done(((f32[128,24]{1,0:T(8,128)}), f32[16,24]{1,0:T(8,128)}) %reduce-scatter.4.cloned.1.call-update) | async-done | bytes 1552
  245.1 0.0 copy-start.2
  245.1 1346.1 %all_gather.3 = f32[24,8192]{0,1:T(8,128)S(1)} all-gather(f32[24,16]{0,1:T(8,128)} %bitcast.54), channel_id=1, replica_groups=mesh['wide'=64,'narrow'=8] {'wide','narrow'}, dimensions={1}, use_global_device_ids=true | all-gather | bytes 787968 | tf_op jit(solution)/shard_map/all_gather | solution.py:75
  1591.1 0.0 copy-done
  1591.1 2.4 fusion.24
  1593.5 0.0 copy-done.4
  1593.5 0.1 reshape.110
  1593.7 19.4 %all_to_all.5 = f32[8,1,384]{2,1,0:T(1,128)S(1)} all-to-all(f32[8,1,384]{2,1,0:T(1,128)S(1)} %reshape.110), channel_id=1, replica_groups=mesh['wide'=64,'narrow'=8] {'narrow'}, dimensions={0} | all-to-all | bytes 24576 | tf_op jit(solution)/shard_map/all_to_all | solution.py:13
  1613.1 0.5 broadcast.96
  1613.6 0.7 reduce
  1614.3 0.1 reshape.111
  1614.4 0.0 copy-done.2
  1614.4 1.0 fusion
  (9 shorter events, 0.1 us)
Async XLA Ops:
  7.2 1584.0 %copy-start = (f32[16,8192]{1,0:T(8,128)S(1)}, f32[16,8192]{1,0:T(8,128)}, u32[]{:S(2)}) copy-start(f32[16,8192]{1,0:T(8,128)} %param.19) | copy-start | bytes 1572868
  7.2 137.4 %copy-start.1 = (f32[4,4,128,128]{3,2,1,0:T(8,128)S(1)}, f32[4,4,128,128]{3,2,1,0:T(8,128)}, u32[]{:S(2)}) copy-start(f32[4,4,128,128]{3,2,1,0:T(8,128)} %param.14) | copy-start | bytes 3145732
  7.2 137.4 %copy-start.3 = (f32[4,128]{1,0:T(4,128)S(1)}, f32[4,128]{1,0:T(4,128)}, u32[]{:S(2)}) copy-start(f32[4,128]{1,0:T(4,128)} %param.13) | copy-start | bytes 6148
  7.2 151.6 %copy-start.5 = (s32[4,128]{1,0:T(4,128)S(1)}, s32[4,128]{1,0:T(4,128)}, u32[]{:S(2)}) copy-start(s32[4,128]{1,0:T(4,128)} %param.18) | copy-start | bytes 6148
  7.2 237.8 %reduce-scatter.4.cloned.1.call-start = ((), (), s32[]{:S(2)}) async-start(), calls=%async_computation.2 | async-start | bytes 73728
  118.5 11.0 collective-permute-start
  120.4 9.1 collective-permute-start.1
  133.0 9.5 collective-permute-start.2
  134.9 9.1 collective-permute-start.3
  146.3 9.5 collective-permute-start.4
  148.2 9.1 collective-permute-start.5
  158.9 1434.7 %copy-start.4 = (f32[4,24,128]{2,1,0:T(8,128)}, f32[4,24,128]{2,1,0:T(8,128)S(1)}, u32[]{:S(2)}) copy-start(f32[4,24,128]{2,1,0:T(8,128)S(1)} %fusion.6) | copy-start | bytes 147460
  245.1 1369.3 %copy-start.2 = (f32[4,24,128]{2,1,0:T(8,128)S(1)}, f32[4,24,128]{2,1,0:T(8,128)}, u32[]{:S(2)}) copy-start(f32[4,24,128]{2,1,0:T(8,128)} %param.12) | copy-start | bytes 147460
Sparse Core Ops, SparseCore 0:
  160.1 84.8 reduce-scatter.3
